TPU v7x, 32 devices: a whole 2x2x4 slice. The times are simulated.
32 devices in a mesh: req: 16 (over z, y, core), grp: 2 (over x).
Axes of the slice: x: 2, y: 2, z: 4, core: 2. Of those that a mesh axis runs over, the one named last changes fastest.
Arguments:
- tokens: bfloat16 [8192, 1024], P('req'), may hold values from -6 to 6
- norm_attn: float32 [1024], replicated, may hold values from 0.25 to 1.75
- w_query: bfloat16 [1024, 1024], P(None, 'grp'), may hold values from -0.1875 to 0.1875
- w_key: bfloat16 [1024, 1024], P(None, 'grp'), may hold values from -0.1875 to 0.1875
- w_value: bfloat16 [1024, 1024], P(None, 'grp'), may hold values from -0.1875 to 0.1875
- w_out: bfloat16 [1024, 1024], P('grp'), may hold values from -0.1875 to 0.1875
- persist_keys: bfloat16 [16, 1024], P(None, 'grp'), may hold values from -5 to 5
- persist_values: bfloat16 [16, 1024], P(None, 'grp'), may hold values from -5 to 5
- kv_cache: bfloat16 [768, 2, 128, 1024], P('req', None, None, 'grp'), may hold values from -160 to 160
- slot_request: int32 [768], P('req'), may hold values from 0 to 255, as said below
- slot_page: int32 [768], P('req'), may hold values from 0 to 48, as said below
- cache_len: int32 [256], P('req'), may hold values from 1 to 2304
- tree_mask: int32 [256, 32, 32], P('req'), may hold values from 0 to 1, as said below
- accept_path: int32 [256, 8], P('req'), may hold values from 0 to 31, as said below
- accept_len: int32 [256], P('req'), may hold values from 1 to 8
- memory: float32 [256, 8, 128, 128], P('req', 'grp'), may hold values from -4 to 4
- momentum: float32 [256, 8, 128, 128], P('req', 'grp'), may hold values from -1.2 to 1.2
- momentum_code: int32 [256, 8, 8], P('req', None, 'grp'), may hold values from 0 to 15
- forget_code: int32 [256, 8, 8], P('req', None, 'grp'), may hold values from 0 to 15
- norm_ffn: float32 [1024], replicated, may hold values from 0.25 to 1.75
- w_gate_up: bfloat16 [2, 1024, 2816], P(None, None, 'grp'), may hold values from -0.1875 to 0.1875
- w_down: bfloat16 [2816, 1024], P('grp'), may hold values from -0.109375 to 0.109375
Outputs:
- layer_out: bfloat16 [8192, 1024], P(('req', 'grp'))
- memory_out: float32 [256, 8, 128, 128], P('req', 'grp')
- momentum_out: float32 [256, 8, 128, 128], P('req', 'grp')
Inputs may be any that keep to these rules, and one draw needn't show every extreme that they name: `slot_request`: slot s lies with index s // 48 of req; slots s with (s % 48) // 3 = j hold pages of requests j * 16 to (j + 1) * 16 - 1 only. The live pages 0 .. ceil(cache_len[r] / 128) - 1 of every request stand each in exactly one slot; every other slot has page number 16 * 3. `slot_page`: see slot_request. `tree_mask`: each node's parent precedes it; node 0 is the root; rows include the node itself. `accept_path`: entry n is the node at depth n on the root path of one draft node.
All inputs are finite; a program needn't handle non-finite values.
Results may differ from a plain program's by a relative error of at most 0.015.
Values may be sent and summed in bfloat16 or wider, within the bound.
No kernel may reach another device: no remote copies, remote signals or barrier semaphores. Data moves between devices by JAX's collectives and lax.ppermute only.
A program may use at most 192 MiB of HBM per device.

v0:
```python
import math
import jax
import jax.numpy as jnp
from jax import lax
from jax.sharding import PartitionSpec as P

HD = 128
EPS = 1e-06
THETA = 0.5
NEG = -1e30


def rms_norm(rows, gain):
    values = rows.astype(jnp.float32)
    factor = lax.rsqrt(jnp.mean(values * values, axis=-1, keepdims=True) + EPS)
    return (values * factor * gain).astype(jnp.bfloat16)


def unit_rows(vectors):
    return vectors * lax.rsqrt(jnp.sum(vectors * vectors, axis=-1, keepdims=True) + EPS)


def page_partials(pages, page_queries, page_first, page_limit, scale):
    count = pages.shape[0]
    page_len = pages.shape[2]
    width = pages.shape[3]
    heads = width // HD
    draft = page_queries.shape[1]
    query_four = page_queries.reshape(count, draft, heads, HD)
    key_four = pages[:, 0].reshape(count, page_len, heads, HD)
    value_four = pages[:, 1].reshape(count, page_len, heads, HD)
    scores = (
        jnp.einsum("sihd,sthd->shit", query_four, key_four, preferred_element_type=jnp.float32)
        * scale
    )
    position = page_first[:, None] + jnp.arange(page_len, dtype=jnp.int32)[None, :]
    valid = (position < page_limit[:, None])[:, None, None, :]
    masked = jnp.where(valid, scores, NEG)
    top = jnp.max(masked, axis=3)
    weight = jnp.where(valid, jnp.exp(masked - top[..., None]), 0.0)
    total = jnp.sum(weight, axis=3)
    numer = jnp.einsum(
        "shit,sthd->sihd",
        weight.astype(jnp.bfloat16),
        value_four,
        preferred_element_type=jnp.float32,
    )
    return (numer.reshape(count, draft, width), top, total)


def on_device(
    tokens,
    norm_attn,
    w_query,
    w_key,
    w_value,
    w_out,
    persist_keys,
    persist_values,
    kv_cache,
    slot_request,
    slot_page,
    cache_len,
    tree_mask,
    accept_path,
    accept_len,
    memory,
    momentum,
    momentum_code,
    forget_code,
    norm_ffn,
    w_gate_up,
    w_down,
):
    group_rows = tokens.shape[0]
    reqs = cache_len.shape[0]
    draft = tree_mask.shape[1]
    width = w_query.shape[1]
    heads = width // HD
    fixed_count = persist_keys.shape[0]
    page_len = kv_cache.shape[2]
    scale = 1.0 / math.sqrt(HD)
    normed = rms_norm(tokens, norm_attn)
    queries = jnp.dot(normed, w_query, preferred_element_type=jnp.float32).astype(jnp.bfloat16)
    keys = jnp.dot(normed, w_key, preferred_element_type=jnp.float32).astype(jnp.bfloat16)
    values = jnp.dot(normed, w_value, preferred_element_type=jnp.float32).astype(jnp.bfloat16)
    query_four = queries.reshape(reqs, draft, heads, HD)
    key_four = keys.reshape(reqs, draft, heads, HD)
    value_four = values.reshape(reqs, draft, heads, HD)
    fixed_keys = persist_keys.reshape(fixed_count, heads, HD)
    fixed_values = persist_values.reshape(fixed_count, heads, HD)
    tree_scores = (
        jnp.einsum("rihd,rjhd->rhij", query_four, key_four, preferred_element_type=jnp.float32)
        * scale
    )
    tree_scores = jnp.where(tree_mask[:, None] == 1, tree_scores, NEG)
    fixed_scores = (
        jnp.einsum("rihd,phd->rhip", query_four, fixed_keys, preferred_element_type=jnp.float32)
        * scale
    )
    local_scores = jnp.concatenate([fixed_scores, tree_scores], axis=3)
    local_top = jnp.max(local_scores, axis=3)
    local_weight = jnp.exp(local_scores - local_top[..., None])
    local_total = jnp.sum(local_weight, axis=3)
    local_rounded = local_weight.astype(jnp.bfloat16)
    local_numer = jnp.einsum(
        "rhip,phd->rihd",
        local_rounded[..., :fixed_count],
        fixed_values,
        preferred_element_type=jnp.float32,
    )
    local_numer = local_numer + jnp.einsum(
        "rhij,rjhd->rihd",
        local_rounded[..., fixed_count:],
        value_four,
        preferred_element_type=jnp.float32,
    )
    first_request = lax.axis_index("req") * reqs
    request_ids = jnp.arange(reqs, dtype=jnp.int32)
    moved_pages, moved_request, moved_page = (
        lax.all_to_all(kv_cache, "req", split_axis=0, concat_axis=0, tiled=True),
        lax.all_to_all(slot_request, "req", split_axis=0, concat_axis=0, tiled=True),
        lax.all_to_all(slot_page, "req", split_axis=0, concat_axis=0, tiled=True),
    )
    local_request = moved_request - first_request
    pick = local_request[:, None] == request_ids[None, :]
    limits = jnp.sum(jnp.where(pick, cache_len[None, :], 0), axis=1)
    page_queries = queries.reshape(reqs, draft, width)[local_request]
    numer, top, total = page_partials(
        moved_pages, page_queries, moved_page * page_len, limits, scale
    )
    slot_count = numer.shape[0]
    pick_weight = pick.astype(jnp.float32)
    request_top = jnp.max(jnp.where(pick[:, :, None, None], top[:, None], NEG), axis=0)
    best = jnp.maximum(request_top, local_top)
    slot_best = jnp.einsum("sr,rhi->shi", pick_weight, best, precision=lax.Precision.HIGHEST)
    factor = jnp.exp(top - slot_best)
    scaled = (
        numer.reshape(slot_count, draft, heads, HD) * jnp.transpose(factor, (0, 2, 1))[..., None]
    )
    page_numer = jnp.einsum("sr,sihd->rihd", pick_weight, scaled, precision=lax.Precision.HIGHEST)
    page_total = jnp.einsum(
        "sr,shi->rhi", pick_weight, total * factor, precision=lax.Precision.HIGHEST
    )
    local_factor = jnp.exp(local_top - best)
    numer_all = local_numer * jnp.transpose(local_factor, (0, 2, 1))[..., None] + page_numer
    total_all = local_total * local_factor + page_total
    attention = numer_all / jnp.transpose(total_all, (0, 2, 1))[..., None]
    unit_query = unit_rows(query_four.astype(jnp.float32))
    retrieved = jnp.einsum("rihd,rhde->rihe", unit_query, memory, precision=lax.Precision.HIGHEST)
    mixed = (attention + retrieved).reshape(group_rows, width).astype(jnp.bfloat16)
    rows = group_rows // lax.axis_size("grp")
    head_sum = lax.psum_scatter(
        jnp.dot(mixed, w_out, preferred_element_type=jnp.float32).astype(jnp.bfloat16),
        "grp",
        scatter_dimension=0,
        tiled=True,
    ).astype(jnp.float32)
    own_rows = lax.dynamic_slice_in_dim(tokens, lax.axis_index("grp") * rows, rows, 0)
    residual = (own_rows.astype(jnp.float32) + head_sum).astype(jnp.bfloat16)
    ffn_in = rms_norm(residual, norm_ffn)
    piece = lax.all_gather(ffn_in, "grp", axis=0, tiled=True)
    gate = jnp.dot(piece, w_gate_up[0], preferred_element_type=jnp.float32)
    up = jnp.dot(piece, w_gate_up[1], preferred_element_type=jnp.float32)
    hidden = (jax.nn.silu(gate) * up).astype(jnp.bfloat16)
    ffn_out = lax.psum_scatter(
        jnp.dot(hidden, w_down, preferred_element_type=jnp.float32).astype(jnp.bfloat16),
        "grp",
        scatter_dimension=0,
        tiled=True,
    ).astype(jnp.float32)
    layer_out = (residual.astype(jnp.float32) + ffn_out).astype(jnp.bfloat16)
    req_rows = request_ids[:, None]
    path_keys = unit_rows(key_four[req_rows, accept_path].astype(jnp.float32))
    path_values = value_four[req_rows, accept_path].astype(jnp.float32)
    eta = 0.97 - 0.06 * momentum_code.astype(jnp.float32)
    forget = 0.01 + 0.02 * forget_code.astype(jnp.float32)
    for step in range(accept_path.shape[1]):
        unit = path_keys[:, step]
        predicted = jnp.einsum("rhd,rhde->rhe", unit, memory, precision=lax.Precision.HIGHEST)
        grad = jnp.einsum(
            "rhd,rhe->rhde", unit, predicted - path_values[:, step], precision=lax.Precision.HIGHEST
        )
        new_mom = eta[:, step, :, None, None] * momentum - THETA * grad
        new_mem = (1.0 - forget[:, step, :, None, None]) * memory + new_mom
        live = (step < accept_len)[:, None, None, None]
        momentum = jnp.where(live, new_mom, momentum)
        memory = jnp.where(live, new_mem, memory)
    return (layer_out, memory, momentum)


def solution(mesh):
    return jax.shard_map(
        on_device,
        mesh=mesh,
        in_specs=(
            P("req", None),
            P(),
            P(None, "grp"),
            P(None, "grp"),
            P(None, "grp"),
            P("grp", None),
            P(None, "grp"),
            P(None, "grp"),
            P("req", None, None, "grp"),
            P("req"),
            P("req"),
            P("req"),
            P("req", None, None),
            P("req", None),
            P("req"),
            P("req", "grp", None, None),
            P("req", "grp", None, None),
            P("req", None, "grp"),
            P("req", None, "grp"),
            P(),
            P(None, None, "grp"),
            P("grp", None),
        ),
        out_specs=(
            P(("req", "grp"), None),
            P("req", "grp", None, None),
            P("req", "grp", None, None),
        ),
        check_vma=False,
    )
```

profile of v0, /device:TPU:0, one launch (start us, length us, event | category | flops | bytes accessed | tf_op | source)
XLA Modules:
  0.0 470.7 jit_solution(17253716148561162837)
XLA Ops:
  8.7 7.4 %all-to-all-start = ((s32[16,3,1]{1,2,0:T(1,128)}), s32[16,3,1]{1,2,0:T(1,128)S(1)}, u32[]{:S(2)}, u32[]{:S(2)}) async-start(s32[16,3,1]{1,2,0:T(1,128)} %bitcast.6), calls=%async_computation | async-start | bytes 16384 | tf_op jit(solution)/shard_map/all_to_all | solution.py:122
  17.4 5.0 %all-to-all-done = s32[16,3,1]{1,2,0:T(1,128)S(1)} async-done(((s32[16,3,1]{1,2,0:T(1,128)}), s32[16,3,1]{1,2,0:T(1,128)S(1)}, u32[]{:S(2)}, u32[]{:S(2)}) %all-to-all-start) | async-done | bytes 224 | tf_op jit(solution)/shard_map/all_to_all | solution.py:122
  25.9 16.7 %copy.234 = bf16[48,2,128,512]{2,3,1,0:T(8,128)(2,1)} copy(bf16[48,2,128,512]{3,2,1,0:T(8,128)(2,1)} %param.30) | data formatting | bytes 25165824 | tf_op args[8]
  43.2 6.0 %all-to-all-start.2 = ((bf16[48,2,128,512]{2,3,1,0:T(8,128)(2,1)}), bf16[48,2,128,512]{2,3,1,0:T(8,128)(2,1)}, u32[]{:S(2)}, u32[]{:S(2)}) async-start(bf16[48,2,128,512]{2,3,1,0:T(8,128)(2,1)} %copy.234), calls=%async_computation.2 | async-start | bytes 25165824 | tf_op jit(solution)/shard_map/all_to_all | solution.py:121
  94.5 5.5 %fusion.145 = f32[16,4,1,128]{3,2,1,0:T(1,128)S(1)} fusion(f32[16,4,128,1]{2,3,1,0:T(1,128)S(1)} %bitcast.263, f32[16,4,128,128]{3,2,1,0:T(8,128)} %param.37), kind=kOutput, calls=%fused_computation.235 | convolution fusion | flops 12582912 | bytes 4259840 | tf_op jit(solution)/shard_map/rhd,rhde->rhe/dot_general | solution.py:180
  100.0 6.6 %fusion.36 = f32[16,4,1,128]{3,2,1,0:T(1,128)S(1)} fusion(f32[16,4,128,1]{2,3,1,0:T(1,128)S(1)} %bitcast.262, f32[16,4,128,128]{3,2,1,0:T(8,128)} %param.37, f32[16,4,128,128]{3,2,1,0:T(8,128)S(1)} %copy-done.1, f32[16,4,128]{2,1,0:T(4,128)S(1)} %fusion.104, f32[16,4,128]{2,1,0:T(4,128)S(1)} %get-tuple-element.14, f32[16,4]{1,0:T(8,128)S(1)} %copy.260, ...), kind=kOutput, calls=%fused_computation.61 | convolution fusion | flops 19922944 | bytes 8520208 | tf_op jit(solution)/shard_map/rhd,rhde->rhe/dot_general | solution.py:180
  114.0 7.9 %fusion.30 = f32[16,4,1,128]{3,2,1,0:T(1,128)S(1)} fusion(f32[16,4,128,1]{2,3,1,0:T(1,128)S(1)} %bitcast.272, f32[16,4,128,128]{3,2,1,0:T(8,128)S(1)} %add_select_fusion.6, f32[16,4,128]{2,1,0:T(4,128)S(1)} %fusion.102, f32[16,4,128]{2,1,0:T(4,128)S(1)} %get-tuple-element.16, f32[16,4]{1,0:T(8,128)S(1)} %copy-done.30, f32[16,4]{1,0:T(8,128)S(1)} %copy-done.50, ...), kind=kOutput, calls=%fused_computation.55 | convolution fusion | flops 30408704 | bytes 8651824 | tf_op jit(solution)/shard_map/rhd,rhde->rhe/dot_general | solution.py:180
  122.0 6.4 %add_select_fusion.4 = f32[16,4,128,128]{3,2,1,0:T(8,128)S(1)} fusion(f32[16,4,128]{2,1,0:T(4,128)S(1)} %fusion.101, f32[16,4,128]{2,1,0:T(4,128)S(1)} %get-tuple-element.17, f32[16,4]{1,0:T(8,128)S(1)} %copy-done.32, f32[16,4,128]{2,1,0:T(4,128)S(1)} %fusion.102, f32[16,4,128,128]{3,2,1,0:T(8,128)S(1)} %add_select_fusion.6, ...), kind=kLoop, calls=%fused_computation.17 | loop fusion | flops 26214400 | bytes 12846656 | tf_op jit(solution)/shard_map/jit(_where)/select_n | solution.py:188
  134.2 5.7 %fusion.6 = f32[16,4,128,128]{3,2,1,0:T(8,128)S(1)} fusion(f32[16,4,128]{2,1,0:T(4,128)S(1)} %fusion.101, f32[16,4,128]{2,1,0:T(4,128)S(1)} %get-tuple-element.17, f32[16,4]{1,0:T(8,128)S(1)} %copy-done.32, f32[16,4,128]{2,1,0:T(4,128)S(1)} %fusion.102, f32[16,4,128]{2,1,0:T(4,128)S(1)} %get-tuple-element.16, f32[16,4]{1,0:T(8,128)S(1)} %copy-done.30, ...), kind=kLoop, calls=%fused_computation.19 | loop fusion | flops 20971520 | bytes 8651840 | tf_op jit(solution)/shard_map/jit(_where)/select_n | solution.py:187
  142.0 4.9 %fusion.27 = f32[16,4,1,128]{3,2,1,0:T(1,128)} fusion(f32[16,4,128,1]{2,3,1,0:T(1,128)S(1)} %bitcast.259, f32[16,4,128,128]{3,2,1,0:T(8,128)S(1)} %add_select_fusion.4, f32[16,4,128,128]{3,2,1,0:T(8,128)S(1)} %fusion.6, f32[16,4,128]{2,1,0:T(4,128)S(1)} %fusion.100, f32[16,4,128]{2,1,0:T(4,128)S(1)} %get-tuple-element.18, f32[16,4]{1,0:T(8,128)S(1)} %copy-done.36, ...), kind=kOutput, calls=%fused_computation.52 | convolution fusion | flops 19922944 | bytes 8520208 | tf_op jit(solution)/shard_map/rhd,rhde->rhe/dot_general | solution.py:180
  161.5 111.4 %all-to-all-done.2 = bf16[48,2,128,512]{2,3,1,0:T(8,128)(2,1)} async-done(((bf16[48,2,128,512]{2,3,1,0:T(8,128)(2,1)}), bf16[48,2,128,512]{2,3,1,0:T(8,128)(2,1)}, u32[]{:S(2)}, u32[]{:S(2)}) %all-to-all-start.2) | async-done | bytes 12582944 | tf_op jit(solution)/shard_map/all_to_all | solution.py:121
  272.9 8.6 %fusion.142 = (bf16[48,1,128,512]{2,3,1,0:T(8,128)(2,1)}, bf16[48,1,128,512]{2,3,1,0:T(8,128)(2,1)S(1)}) fusion(bf16[48,2,128,512]{2,3,1,0:T(8,128)(2,1)} %all-to-all-done.2), kind=kLoop, calls=%fused_computation.232 | loop fusion | bytes 25165824 | tf_op jit(solution)/shard_map/slice | solution.py:31
  281.6 4.1 fusion.18
  293.7 4.6 fusion.19
  298.3 5.9 %bitcast_multiply_fusion = f32[48,32,4,128]{3,1,2,0:T(8,128)S(1)} fusion(bf16[48,128,4,128]{1,3,2,0:T(8,128)(2,1)} %bitcast.250, f32[48,4,32,128]{3,2,1,0:T(8,128)S(1)} %copy-done.6, f32[48,32,4]{1,2,0:T(4,128)} %copy.244, f32[48,4,32]{2,1,0:T(4,128)} %get-tuple-element.53, pred[48,128]{1,0:T(8,128)(4,1)} %add_compare_fusion), kind=kOutput, calls=%fused_computation.30 | convolution fusion | flops 206045184 | bytes 12638208 | tf_op jit(solution)/shard_map/shit,sthd->sihd/dot_general | solution.py:42
  304.3 4.7 fusion.10
  325.9 10.3 %add_select_fusion.2 = f32[16,4,128,128]{3,2,1,0:T(8,128)S(1)} fusion(f32[16,4,128]{2,1,0:T(4,128)S(1)} %fusion.99, f32[16,4,128]{2,1,0:T(4,128)S(1)} %copy-done.26, f32[16,4]{1,0:T(8,128)S(1)} %copy.271, f32[16,4,128]{2,1,0:T(4,128)S(1)} %copy-done.22, f32[16,4,128,128]{3,2,1,0:T(8,128)} %copy-done.4, f32[16,4,128]{2,1,0:T(4,128)S(1)} %copy-done.20, ...), kind=kLoop, calls=%fused_computation.11 | loop fusion | flops 36700160 | bytes 12978272 | tf_op jit(solution)/shard_map/jit(_where)/select_n | solution.py:188
  343.3 48.5 %reduce-scatter.3.cloned.1.call-done = bf16[256,1024]{1,0:T(8,128)(2,1)} async-done(((bf16[512,1024]{1,0:T(8,128)(2,1)}), bf16[256,1024]{1,0:T(8,128)(2,1)}) %reduce-scatter.3.cloned.1.call-update) | async-done | bytes 524304 | tf_op jit(solution)/shard_map/reduce_scatter | solution.py:153
  395.0 9.2 %fusion.24 = f32[16,4,1,128]{3,2,1,0:T(1,128)S(1)} fusion(f32[16,4,128,1]{2,3,1,0:T(1,128)} %bitcast.271, f32[16,4,128,128]{3,2,1,0:T(8,128)} %copy-done.5, f32[16,4,128]{2,1,0:T(4,128)} %fusion.98, f32[16,4,128]{2,1,0:T(4,128)} %get-tuple-element.20, f32[16,4]{1,0:T(8,128)} %copy.273, f32[16,4]{1,0:T(8,128)} %copy.253, ...), kind=kOutput, calls=%fused_computation.49 | convolution fusion | flops 30408704 | bytes 8651824 | tf_op jit(solution)/shard_map/rhd,rhde->rhe/dot_general | solution.py:180
  405.6 11.0 %all-gather.2.cloned.1.call-done = bf16[512,1024]{1,0:T(8,128)(2,1)} async-done(((bf16[256,1024]{1,0:T(8,128)(2,1)}), bf16[512,1024]{1,0:T(8,128)(2,1)}) %all-gather.2.cloned.1.call-update) | async-done | bytes 1048592 | tf_op jit(solution)/shard_map/all_gather | solution.py:162
  416.6 5.5 %fusion.14 = f32[512,1408]{1,0:T(8,128)} fusion(bf16[512,1024]{1,0:T(8,128)(2,1)} %all-gather.2.cloned.1.call-done, bf16[2,1024,1408]{2,1,0:T(8,128)(2,1)} %param.42), kind=kOutput, calls=%fused_computation.37 | convolution fusion | flops 1476395008 | bytes 6815744 | tf_op jit(solution)/shard_map/dot_general | solution.py:163
  422.1 7.4 %convolution_convert_fusion = bf16[512,1024]{1,0:T(8,128)(2,1)} fusion(bf16[1408,1024]{1,0:T(8,128)(2,1)S(1)} %copy-done, bf16[512,1024]{1,0:T(8,128)(2,1)} %all-gather.2.cloned.1.call-done, bf16[2,1024,1408]{2,1,0:T(8,128)(2,1)} %param.42, f32[512,1408]{1,0:T(8,128)} %fusion.14), kind=kOutput, calls=%fused_computation.84 | convolution fusion | flops 2957639680 | bytes 10747904 | tf_op jit(solution)/shard_map/dot_general | solution.py:167
  429.6 15.2 %fusion.2 = f32[16,4,128,128]{3,2,1,0:T(8,128)} fusion(f32[16,4,128]{2,1,0:T(4,128)} %fusion.97, f32[16,4,128]{2,1,0:T(4,128)} %get-tuple-element.13, f32[16,4]{1,0:T(8,128)} %copy.275, f32[16,4,128]{2,1,0:T(4,128)} %fusion.98, f32[16,4,128]{2,1,0:T(4,128)} %get-tuple-element.20, f32[16,4]{1,0:T(8,128)} %copy.273, pred[16]{0:T(512)(128)(4,1)} %get-tuple-element.50, ...), kind=kLoop, calls=%fused_computation.7 | loop fusion | flops 41943040 | bytes 8915072 | tf_op jit(solution)/shard_map/jit(_where)/select_n | solution.py:187
  446.1 15.8 %add_select_fusion = f32[16,4,128,128]{3,2,1,0:T(8,128)} fusion(f32[16,4,128]{2,1,0:T(4,128)} %fusion.97, f32[16,4,128]{2,1,0:T(4,128)} %get-tuple-element.13, f32[16,4]{1,0:T(8,128)} %copy.275, f32[16,4,128]{2,1,0:T(4,128)} %fusion.98, f32[16,4,128,128]{3,2,1,0:T(8,128)} %copy-done.5, f32[16,4,128]{2,1,0:T(4,128)} %get-tuple-element.20, f32[16,4]{1,0:T(8,128)} %copy.273, ...), kind=kLoop, calls=%fused_computation.5 | loop fusion | flops 47185920 | bytes 13109888 | tf_op jit(solution)/shard_map/jit(_where)/select_n | solution.py:188
  (242 shorter events, 121.3 us)
Async XLA Ops:
  7.2 414.9 %copy-start = (bf16[1408,1024]{1,0:T(8,128)(2,1)S(1)}, bf16[1408,1024]{1,0:T(8,128)(2,1)}, u32[]{:S(2)}) copy-start(bf16[1408,1024]{1,0:T(8,128)(2,1)} %param.43) | copy-start | bytes 8650756
  8.7 13.7 %all-to-all-start = ((s32[16,3,1]{1,2,0:T(1,128)}), s32[16,3,1]{1,2,0:T(1,128)S(1)}, u32[]{:S(2)}, u32[]{:S(2)}) async-start(s32[16,3,1]{1,2,0:T(1,128)} %bitcast.6), calls=%async_computation | async-start | bytes 16384 | tf_op jit(solution)/shard_map/all_to_all | solution.py:122
  22.4 20.1 %copy-start.48 = (s32[16,3,1]{1,2,0:T(1,128)}, s32[16,3,1]{1,2,0:T(1,128)S(1)}, u32[]{:S(2)}) copy-start(s32[16,3,1]{1,2,0:T(1,128)S(1)} %all-to-all-done) | copy-start | bytes 580
  22.4 20.2 %all-to-all-start.1 = ((s32[16,3,1]{1,2,0:T(1,128)}), s32[16,3,1]{1,2,0:T(1,128)S(1)}, u32[]{:S(2)}, u32[]{:S(2)}) async-start(s32[16,3,1]{1,2,0:T(1,128)} %bitcast.7), calls=%async_computation.1 | async-start | bytes 16384 | tf_op jit(solution)/shard_map/all_to_all | solution.py:123
  43.2 229.8 %all-to-all-start.2 = ((bf16[48,2,128,512]{2,3,1,0:T(8,128)(2,1)}), bf16[48,2,128,512]{2,3,1,0:T(8,128)(2,1)}, u32[]{:S(2)}, u32[]{:S(2)}) async-start(bf16[48,2,128,512]{2,3,1,0:T(8,128)(2,1)} %copy.234), calls=%async_computation.2 | async-start | bytes 25165824 | tf_op jit(solution)/shard_map/all_to_all | solution.py:121
  49.2 342.6 %reduce-scatter.3.cloned.1.call-start = ((), (), s32[]{:S(2)}) async-start(), calls=%async_computation.5 | async-start | bytes 1572864 | tf_op jit(solution)/shard_map/reduce_scatter | solution.py:153
  58.8 11.6 %copy-start.68 = (s32[16,8]{0,1:T(8,128)S(1)}, s32[16,8]{0,1:T(8,128)}, u32[]{:S(2)}) copy-start(s32[16,8]{0,1:T(8,128)} %param.35) | copy-start | bytes 1540
  90.8 9.2 %copy-start.1 = (f32[16,4,128,128]{3,2,1,0:T(8,128)S(1)}, f32[16,4,128,128]{3,2,1,0:T(8,128)}, u32[]{:S(2)}) copy-start(f32[16,4,128,128]{3,2,1,0:T(8,128)} %param.38) | copy-start | bytes 12582916
  90.8 9.2 %copy-start.44 = (f32[16,4]{1,0:T(8,128)S(1)}, f32[16,4]{1,0:T(8,128)}, u32[]{:S(2)}) copy-start(f32[16,4]{1,0:T(8,128)} %copy.259) | copy-start | bytes 772
  92.9 41.3 %copy-start.52 = (pred[16]{0:T(512)(128)(4,1)}, pred[16]{0:T(512)(128)(4,1)S(1)}, u32[]{:S(2)}) copy-start(pred[16]{0:T(512)(128)(4,1)S(1)} %get-tuple-element.52) | copy-start | bytes 52
  92.9 41.3 %copy-start.54 = (pred[16]{0:T(512)(128)(4,1)}, pred[16]{0:T(512)(128)(4,1)S(1)}, u32[]{:S(2)}) copy-start(pred[16]{0:T(512)(128)(4,1)S(1)} %get-tuple-element.46) | copy-start | bytes 52
  92.9 41.3 %copy-start.56 = (pred[16]{0:T(512)(128)(4,1)}, pred[16]{0:T(512)(128)(4,1)S(1)}, u32[]{:S(2)}) copy-start(pred[16]{0:T(512)(128)(4,1)S(1)} %get-tuple-element.47) | copy-start | bytes 52
  92.9 47.1 %copy-start.60 = (pred[16]{0:T(512)(128)(4,1)}, pred[16]{0:T(512)(128)(4,1)S(1)}, u32[]{:S(2)}) copy-start(pred[16]{0:T(512)(128)(4,1)S(1)} %get-tuple-element.48) | copy-start | bytes 52
  94.5 39.7 %copy-start.9 = (f32[16,4,128]{2,1,0:T(4,128)}, f32[16,4,128]{2,1,0:T(4,128)S(1)}, u32[]{:S(2)}) copy-start(f32[16,4,128]{2,1,0:T(4,128)S(1)} %get-tuple-element.16) | copy-start | bytes 98308
  94.5 39.7 %copy-start.11 = (f32[16,4,128]{2,1,0:T(4,128)}, f32[16,4,128]{2,1,0:T(4,128)S(1)}, u32[]{:S(2)}) copy-start(f32[16,4,128]{2,1,0:T(4,128)S(1)} %get-tuple-element.17) | copy-start | bytes 98308
  94.5 45.5 %copy-start.19 = (f32[16,4,128]{2,1,0:T(4,128)}, f32[16,4,128]{2,1,0:T(4,128)S(1)}, u32[]{:S(2)}) copy-start(f32[16,4,128]{2,1,0:T(4,128)S(1)} %get-tuple-element.18) | copy-start | bytes 98308
  113.9 20.2 %copy-start.13 = (f32[16,4,128]{2,1,0:T(4,128)}, f32[16,4,128]{2,1,0:T(4,128)S(1)}, u32[]{:S(2)}) copy-start(f32[16,4,128]{2,1,0:T(4,128)S(1)} %fusion.102) | copy-start | bytes 98308
  122.0 12.2 %copy-start.15 = (f32[16,4,128]{2,1,0:T(4,128)}, f32[16,4,128]{2,1,0:T(4,128)S(1)}, u32[]{:S(2)}) copy-start(f32[16,4,128]{2,1,0:T(4,128)S(1)} %fusion.101) | copy-start | bytes 98308
  128.4 11.6 %copy-start.4 = (f32[16,4,128,128]{3,2,1,0:T(8,128)}, f32[16,4,128,128]{3,2,1,0:T(8,128)S(1)}, u32[]{:S(2)}) copy-start(f32[16,4,128,128]{3,2,1,0:T(8,128)S(1)} %add_select_fusion.4) | copy-start | bytes 12582916
  322.7 93.9 %all-gather.2.cloned.1.call-start = ((), (), s32[]{:S(2)}) async-start(), calls=%async_computation.6 | async-start | bytes 1572864 | tf_op jit(solution)/shard_map/all_gather | solution.py:162
  323.5 12.7 %copy-start.27 = (f32[16,4,128]{2,1,0:T(4,128)}, f32[16,4,128]{2,1,0:T(4,128)S(1)}, u32[]{:S(2)}) copy-start(f32[16,4,128]{2,1,0:T(4,128)S(1)} %fusion.99) | copy-start | bytes 98308
  323.6 12.6 %copy-start.42 = (f32[16,4]{1,0:T(8,128)}, f32[16,4]{1,0:T(8,128)S(1)}, u32[]{:S(2)}) copy-start(f32[16,4]{1,0:T(8,128)S(1)} %copy.271) | copy-start | bytes 772
  325.9 12.4 %copy-start.38 = (f32[16,1,4,128]{3,2,1,0:T(4,128)S(1)}, f32[16,1,4,128]{3,2,1,0:T(4,128)}, u32[]{:S(2)}) copy-start(f32[16,1,4,128]{3,2,1,0:T(4,128)} %get-tuple-element.22) | copy-start | bytes 98308
  395.0 66.9 %reduce-scatter.5.cloned.1.call-start = ((), (), s32[]{:S(2)}) async-start(), calls=%async_computation.7 | async-start | bytes 1572864 | tf_op jit(solution)/shard_map/reduce_scatter | solution.py:166
  (53 other events, 276.1 us)
Sparse Core Ops, SparseCore 0:
  322.8 68.9 reduce-scatter.2
  395.1 21.4 all-gather.1
  429.7 20.3 reduce-scatter.4
where the time goes:
time: 478 us; the launch traced here: 471 us
  waiting for transfers between devices  176 us (37%)
  matrix products  96.6 us (20%)
  other arithmetic  91.4 us (19%)
  local copies, waits for them, and re-layouts  74.8 us (16%)
  starting transfers between devices  17 us (4%)
  between operations  15 us (3%)
    all_to_all x1, waiting for transfers between devices, on_device(): lax.all_to_all(kv_cache, 'req', split_axis=0, concat_axis=0, tiled=True)  111 us
    reduce_scatter x1, waiting for transfers between devices, on_device(): lax.psum_scatter(jnp.dot(mixed, w_out, preferred_element_type=jnp.float32...  48.5 us
    dot_general x8, matrix products, on_device(): jnp.einsum('rhd,rhde->rhe', unit, memory, precision=lax.Precision.HIGHEST)  45.1 us
    select_n x4, other arithmetic, on_device(): memory = jnp.where(live, new_mem, memory)  36 us
    unnamed x143, local copies, waits for them, and re-layouts  21.6 us
    select_n x2, other arithmetic, on_device(): momentum = jnp.where(live, new_mom, momentum)  20.9 us
    all_gather x1, waiting for transfers between devices, on_device(): piece = lax.all_gather(ffn_in, 'grp', axis=0, tiled=True)  11 us
  transfers between devices with their start and end apart: 6, of which 4 were waited for; matrix products, arithmetic and copies ran while one was open for 40% of the time, Pallas kernels for 0%

commit v1 on v0

--- a/solution.py
+++ b/solution.py
@@ -8,6 +8,29 @@
 EPS = 1e-06
 THETA = 0.5
 NEG = -1e30
+
+
+def in_blocks(x, dim, peers):
+    shape = x.shape
+    tiles = x.reshape(*shape[:dim], peers, shape[dim] // peers, *shape[dim + 1 :])
+    return jnp.moveaxis(tiles, dim, 0)
+
+
+def laid_out(blocks, dim):
+    blocks = jnp.moveaxis(blocks, 0, dim)
+    shape = blocks.shape
+    return blocks.reshape(*shape[:dim], shape[dim] * shape[dim + 1], *shape[dim + 2 :])
+
+
+def exchange_in_pairs(x, axis, split_dim, concat_dim):
+    size, position = (lax.axis_size(axis), lax.axis_index(axis))
+    tiles = in_blocks(x, split_dim, size)
+    finished = [tiles[position]]
+    for hop in range(1, size):
+        sent = tiles[position ^ hop]
+        finished.append(lax.ppermute(sent, axis, [(i, i ^ hop) for i in range(size)]))
+    tiles = jnp.stack(finished)[position ^ jnp.arange(size)]
+    return laid_out(tiles, concat_dim)
 
 
 def rms_norm(rows, gain):
@@ -119,7 +142,7 @@
     request_ids = jnp.arange(reqs, dtype=jnp.int32)
     moved_pages, moved_request, moved_page = (
         lax.all_to_all(kv_cache, "req", split_axis=0, concat_axis=0, tiled=True),
-        lax.all_to_all(slot_request, "req", split_axis=0, concat_axis=0, tiled=True),
+        exchange_in_pairs(slot_request, "req", 0, 0),
         lax.all_to_all(slot_page, "req", split_axis=0, concat_axis=0, tiled=True),
     )
     local_request = moved_request - first_request

time: 478 us -> 490 us (1.025)
  starting transfers between devices: 17 us -> 36.6 us
    ppermute x0 -> x15, waiting for transfers between devices: none -> 163 us  [exchange_in_pairs(): lax.ppermute(sent, axis, [(i, i ^ hop) for i in range(size)])]
    all_to_all x1, waiting for transfers between devices: 111 us -> 0.01 us  [on_device(): lax.all_to_all(kv_cache, 'req', split_axis=0, concat_axis=0, tiled=True)]
    reduce_scatter x1, waiting for transfers between devices: 48.5 us -> 0.01 us  [on_device(): lax.psum_scatter(jnp.dot(mixed, w_out, preferred_element_type=jnp.float32...]
    ppermute x0 -> x15, starting transfers between devices: none -> 23 us  [exchange_in_pairs(): lax.ppermute(sent, axis, [(i, i ^ hop) for i in range(size)])]
    all_to_all x1 -> x0, starting transfers between devices: 7.39 us -> none  [on_device(): lax.all_to_all(slot_request, 'req', split_axis=0, concat_axis=0, tiled=True)]
    all_to_all x1 -> x0, waiting for transfers between devices: 4.99 us -> none  [on_device(): lax.all_to_all(slot_request, 'req', split_axis=0, concat_axis=0, tiled=True)]
    unnamed x143 -> x185, local copies, waits for them, and re-layouts: 21.6 us -> 20.1 us
  transfers between devices with their start and end apart: 6 -> 20, of which waited for: 4 -> 5; matrix products, arithmetic and copies ran while one was open for 40% -> 38% of each run, Pallas kernels for 0% -> 0%
where the time goes in v1:
time: 490 us; the launch traced here: 482 us
  waiting for transfers between devices  173 us (35%)
  matrix products  96.6 us (20%)
  other arithmetic  87.9 us (18%)
  local copies, waits for them, and re-layouts  73 us (15%)
  starting transfers between devices  36.6 us (7%)
  between operations  15.4 us (3%)
    ppermute x15, waiting for transfers between devices, exchange_in_pairs(): lax.ppermute(sent, axis, [(i, i ^ hop) for i in range(size)])  163 us
    dot_general x8, matrix products, on_device(): jnp.einsum('rhd,rhde->rhe', unit, memory, precision=lax.Precision.HIGHEST)  45.1 us
    select_n x4, other arithmetic, on_device(): memory = jnp.where(live, new_mem, memory)  36 us
    ppermute x15, starting transfers between devices, exchange_in_pairs(): lax.ppermute(sent, axis, [(i, i ^ hop) for i in range(size)])  23 us
    select_n x2, other arithmetic, on_device(): momentum = jnp.where(live, new_mom, momentum)  20.9 us
    unnamed x185, local copies, waits for them, and re-layouts  20.1 us
  transfers between devices with their start and end apart: 20, of which 5 were waited for; matrix products, arithmetic and copies ran while one was open for 38% of the time, Pallas kernels for 0%

profile of v1, /device:TPU:0, one launch (start us, length us, event | category | flops | bytes accessed | tf_op | source)
XLA Modules:
  0.0 482.1 jit_solution(10953448743270184360)
XLA Ops:
  8.7 7.4 %all-to-all-start = ((s32[16,3,1]{1,2,0:T(1,128)}), s32[16,3,1]{1,2,0:T(1,128)S(1)}, u32[]{:S(2)}, u32[]{:S(2)}) async-start(s32[16,3,1]{1,2,0:T(1,128)} %bitcast.37), calls=%async_computation | async-start | bytes 16384 | tf_op jit(solution)/shard_map/all_to_all | solution.py:146
  16.1 16.7 %copy.265 = bf16[48,2,128,512]{2,3,1,0:T(8,128)(2,1)} copy(bf16[48,2,128,512]{3,2,1,0:T(8,128)(2,1)} %param.30) | data formatting | bytes 25165824 | tf_op args[8]
  33.3 6.0 %all-to-all-start.1 = ((bf16[48,2,128,512]{2,3,1,0:T(8,128)(2,1)}), bf16[48,2,128,512]{2,3,1,0:T(8,128)(2,1)}, u32[]{:S(2)}, u32[]{:S(2)}) async-start(bf16[48,2,128,512]{2,3,1,0:T(8,128)(2,1)} %copy.265), calls=%async_computation.1 | async-start | bytes 25165824 | tf_op jit(solution)/shard_map/all_to_all | solution.py:144
  89.7 5.5 %fusion.160 = f32[16,4,1,128]{3,2,1,0:T(1,128)S(1)} fusion(f32[16,4,128,1]{2,3,1,0:T(1,128)S(1)} %bitcast.307, f32[16,4,128,128]{3,2,1,0:T(8,128)} %param.37), kind=kOutput, calls=%fused_computation.269 | convolution fusion | flops 12582912 | bytes 4259840 | tf_op jit(solution)/shard_map/rhd,rhde->rhe/dot_general | solution.py:203
  95.2 6.6 %fusion.36 = f32[16,4,1,128]{3,2,1,0:T(1,128)S(1)} fusion(f32[16,4,128,1]{2,3,1,0:T(1,128)S(1)} %bitcast.306, f32[16,4,128,128]{3,2,1,0:T(8,128)} %param.37, f32[16,4,128,128]{3,2,1,0:T(8,128)S(1)} %copy-done.1, f32[16,4,128]{2,1,0:T(4,128)S(1)} %fusion.104, f32[16,4,128]{2,1,0:T(4,128)S(1)} %get-tuple-element.12, f32[16,4]{1,0:T(8,128)S(1)} %copy.291, ...), kind=kOutput, calls=%fused_computation.62 | convolution fusion | flops 19922944 | bytes 8520208 | tf_op jit(solution)/shard_map/rhd,rhde->rhe/dot_general | solution.py:203
  109.2 7.9 %fusion.30 = f32[16,4,1,128]{3,2,1,0:T(1,128)S(1)} fusion(f32[16,4,128,1]{2,3,1,0:T(1,128)S(1)} %bitcast.316, f32[16,4,128,128]{3,2,1,0:T(8,128)S(1)} %add_select_fusion.6, f32[16,4,128]{2,1,0:T(4,128)S(1)} %fusion.102, f32[16,4,128]{2,1,0:T(4,128)S(1)} %get-tuple-element.14, f32[16,4]{1,0:T(8,128)S(1)} %copy-done.32, f32[16,4]{1,0:T(8,128)S(1)} %copy-done.50, ...), kind=kOutput, calls=%fused_computation.56 | convolution fusion | flops 30408704 | bytes 8651824 | tf_op jit(solution)/shard_map/rhd,rhde->rhe/dot_general | solution.py:203
  117.2 6.4 %add_select_fusion.4 = f32[16,4,128,128]{3,2,1,0:T(8,128)S(1)} fusion(f32[16,4,128]{2,1,0:T(4,128)S(1)} %fusion.101, f32[16,4,128]{2,1,0:T(4,128)S(1)} %get-tuple-element.15, f32[16,4]{1,0:T(8,128)S(1)} %copy-done.34, f32[16,4,128]{2,1,0:T(4,128)S(1)} %fusion.102, f32[16,4,128,128]{3,2,1,0:T(8,128)S(1)} %add_select_fusion.6, ...), kind=kLoop, calls=%fused_computation.18 | loop fusion | flops 26214400 | bytes 12846656 | tf_op jit(solution)/shard_map/jit(_where)/select_n | solution.py:211
  129.5 5.7 %fusion.6 = f32[16,4,128,128]{3,2,1,0:T(8,128)S(1)} fusion(f32[16,4,128]{2,1,0:T(4,128)S(1)} %fusion.101, f32[16,4,128]{2,1,0:T(4,128)S(1)} %get-tuple-element.15, f32[16,4]{1,0:T(8,128)S(1)} %copy-done.34, f32[16,4,128]{2,1,0:T(4,128)S(1)} %fusion.102, f32[16,4,128]{2,1,0:T(4,128)S(1)} %get-tuple-element.14, f32[16,4]{1,0:T(8,128)S(1)} %copy-done.32, ...), kind=kLoop, calls=%fused_computation.20 | loop fusion | flops 20971520 | bytes 8651840 | tf_op jit(solution)/shard_map/jit(_where)/select_n | solution.py:210
  135.4 4.9 %fusion.27 = f32[16,4,1,128]{3,2,1,0:T(1,128)} fusion(f32[16,4,128,1]{2,3,1,0:T(1,128)S(1)} %bitcast.303, f32[16,4,128,128]{3,2,1,0:T(8,128)S(1)} %add_select_fusion.4, f32[16,4,128,128]{3,2,1,0:T(8,128)S(1)} %fusion.6, f32[16,4,128]{2,1,0:T(4,128)S(1)} %fusion.100, f32[16,4,128]{2,1,0:T(4,128)S(1)} %get-tuple-element.16, f32[16,4]{1,0:T(8,128)S(1)} %copy-done.38, ...), kind=kOutput, calls=%fused_computation.53 | convolution fusion | flops 19922944 | bytes 8520208 | tf_op jit(solution)/shard_map/rhd,rhde->rhe/dot_general | solution.py:203
  145.6 97.3 %collective-permute-done.3 = s32[3]{0:T(128)} collective-permute-done((s32[3]{0:T(128)}, s32[3]{0:T(128)}, u32[]{:S(2)}, u32[]{:S(2)}) %collective-permute-start.3) | collective-permute-done | bytes 44 | tf_op jit(solution)/shard_map/ppermute | solution.py:31
  251.2 62.1 %collective-permute-done.7 = s32[3]{0:T(128)S(1)} collective-permute-done((s32[3]{0:T(128)S(1)}, s32[3]{0:T(128)S(1)}, u32[]{:S(2)}, u32[]{:S(2)}) %collective-permute-start.7) | collective-permute-done | bytes 44 | tf_op jit(solution)/shard_map/ppermute | solution.py:31
  334.7 8.8 %fusion.157 = (bf16[48,1,128,512]{2,3,1,0:T(8,128)(2,1)}, bf16[48,1,128,512]{2,3,1,0:T(8,128)(2,1)S(1)}) fusion(bf16[48,2,128,512]{2,3,1,0:T(8,128)(2,1)} %all-to-all-done.1), kind=kLoop, calls=%fused_computation.266 | loop fusion | bytes 25165824 | tf_op jit(solution)/shard_map/slice | solution.py:54
  343.5 4.1 fusion.18
  355.7 4.1 fusion.19
  359.8 5.9 %bitcast_multiply_fusion = f32[48,32,4,128]{3,1,2,0:T(8,128)S(1)} fusion(bf16[48,128,4,128]{1,3,2,0:T(8,128)(2,1)} %bitcast.294, f32[48,4,32,128]{3,2,1,0:T(8,128)S(1)} %copy-done.6, f32[48,32,4]{1,2,0:T(4,128)} %copy.275, f32[48,4,32]{2,1,0:T(4,128)} %get-tuple-element.67, pred[48,128]{1,0:T(8,128)(4,1)S(1)} %add_compare_fusion), kind=kOutput, calls=%fused_computation.31 | convolution fusion | flops 206045184 | bytes 12638208 | tf_op jit(solution)/shard_map/shit,sthd->sihd/dot_general | solution.py:65
  365.7 4.7 fusion.10
  377.8 3.9 fusion.70
  387.3 10.3 %add_select_fusion.2 = f32[16,4,128,128]{3,2,1,0:T(8,128)S(1)} fusion(f32[16,4,128]{2,1,0:T(4,128)S(1)} %fusion.99, f32[16,4,128]{2,1,0:T(4,128)S(1)} %copy-done.26, f32[16,4]{1,0:T(8,128)S(1)} %copy.302, f32[16,4,128]{2,1,0:T(4,128)S(1)} %copy-done.22, f32[16,4,128,128]{3,2,1,0:T(8,128)} %copy-done.4, f32[16,4,128]{2,1,0:T(4,128)S(1)} %copy-done.20, ...), kind=kLoop, calls=%fused_computation.12 | loop fusion | flops 36700160 | bytes 12978272 | tf_op jit(solution)/shard_map/jit(_where)/select_n | solution.py:211
  408.0 9.2 %fusion.24 = f32[16,4,1,128]{3,2,1,0:T(1,128)S(1)} fusion(f32[16,4,128,1]{2,3,1,0:T(1,128)} %bitcast.315, f32[16,4,128,128]{3,2,1,0:T(8,128)} %copy-done.5, f32[16,4,128]{2,1,0:T(4,128)} %fusion.98, f32[16,4,128]{2,1,0:T(4,128)} %get-tuple-element.18, f32[16,4]{1,0:T(8,128)} %copy.304, f32[16,4]{1,0:T(8,128)} %copy.284, ...), kind=kOutput, calls=%fused_computation.50 | convolution fusion | flops 30408704 | bytes 8651824 | tf_op jit(solution)/shard_map/rhd,rhde->rhe/dot_general | solution.py:203
  418.6 9.4 %all-gather.2.cloned.1.call-done = bf16[512,1024]{1,0:T(8,128)(2,1)} async-done(((bf16[256,1024]{1,0:T(8,128)(2,1)}), bf16[512,1024]{1,0:T(8,128)(2,1)}) %all-gather.2.cloned.1.call-update) | async-done | bytes 1048592 | tf_op jit(solution)/shard_map/all_gather | solution.py:185
  428.0 5.5 %fusion.14 = f32[512,1408]{1,0:T(8,128)} fusion(bf16[512,1024]{1,0:T(8,128)(2,1)} %all-gather.2.cloned.1.call-done, bf16[2,1024,1408]{2,1,0:T(8,128)(2,1)} %param.42), kind=kOutput, calls=%fused_computation.38 | convolution fusion | flops 1476395008 | bytes 6815744 | tf_op jit(solution)/shard_map/dot_general | solution.py:186
  433.5 7.4 %convolution_convert_fusion = bf16[512,1024]{1,0:T(8,128)(2,1)} fusion(bf16[1408,1024]{1,0:T(8,128)(2,1)S(1)} %copy-done, bf16[512,1024]{1,0:T(8,128)(2,1)} %all-gather.2.cloned.1.call-done, bf16[2,1024,1408]{2,1,0:T(8,128)(2,1)} %param.42, f32[512,1408]{1,0:T(8,128)} %fusion.14), kind=kOutput, calls=%fused_computation.85 | convolution fusion | flops 2957639680 | bytes 10747904 | tf_op jit(solution)/shard_map/dot_general | solution.py:190
  441.0 15.2 %fusion.2 = f32[16,4,128,128]{3,2,1,0:T(8,128)} fusion(f32[16,4,128]{2,1,0:T(4,128)} %fusion.97, f32[16,4,128]{2,1,0:T(4,128)} %get-tuple-element.11, f32[16,4]{1,0:T(8,128)} %copy.306, f32[16,4,128]{2,1,0:T(4,128)} %fusion.98, f32[16,4,128]{2,1,0:T(4,128)} %get-tuple-element.18, f32[16,4]{1,0:T(8,128)} %copy.304, pred[16]{0:T(512)(128)(4,1)} %get-tuple-element.64, ...), kind=kLoop, calls=%fused_computation.8 | loop fusion | flops 41943040 | bytes 8915072 | tf_op jit(solution)/shard_map/jit(_where)/select_n | solution.py:210
  457.6 15.8 %add_select_fusion = f32[16,4,128,128]{3,2,1,0:T(8,128)} fusion(f32[16,4,128]{2,1,0:T(4,128)} %fusion.97, f32[16,4,128]{2,1,0:T(4,128)} %get-tuple-element.11, f32[16,4]{1,0:T(8,128)} %copy.306, f32[16,4,128]{2,1,0:T(4,128)} %fusion.98, f32[16,4,128,128]{3,2,1,0:T(8,128)} %copy-done.5, f32[16,4,128]{2,1,0:T(4,128)} %get-tuple-element.18, f32[16,4]{1,0:T(8,128)} %copy.304, ...), kind=kLoop, calls=%fused_computation.6 | loop fusion | flops 47185920 | bytes 13109888 | tf_op jit(solution)/shard_map/jit(_where)/select_n | solution.py:211
  (316 shorter events, 135.8 us)
Async XLA Ops:
  7.2 426.4 %copy-start = (bf16[1408,1024]{1,0:T(8,128)(2,1)S(1)}, bf16[1408,1024]{1,0:T(8,128)(2,1)}, u32[]{:S(2)}) copy-start(bf16[1408,1024]{1,0:T(8,128)(2,1)} %param.43) | copy-start | bytes 8650756
  8.7 24.1 %all-to-all-start = ((s32[16,3,1]{1,2,0:T(1,128)}), s32[16,3,1]{1,2,0:T(1,128)S(1)}, u32[]{:S(2)}, u32[]{:S(2)}) async-start(s32[16,3,1]{1,2,0:T(1,128)} %bitcast.37), calls=%async_computation | async-start | bytes 16384 | tf_op jit(solution)/shard_map/all_to_all | solution.py:146
  33.3 301.3 %all-to-all-start.1 = ((bf16[48,2,128,512]{2,3,1,0:T(8,128)(2,1)}), bf16[48,2,128,512]{2,3,1,0:T(8,128)(2,1)}, u32[]{:S(2)}, u32[]{:S(2)}) async-start(bf16[48,2,128,512]{2,3,1,0:T(8,128)(2,1)} %copy.265), calls=%async_computation.1 | async-start | bytes 25165824 | tf_op jit(solution)/shard_map/all_to_all | solution.py:144
  39.4 365.3 %reduce-scatter.3.cloned.1.call-start = ((), (), s32[]{:S(2)}) async-start(), calls=%async_computation.4 | async-start | bytes 1572864 | tf_op jit(solution)/shard_map/reduce_scatter | solution.py:176
  40.4 100.0 %collective-permute-start = (s32[3]{0:T(128)}, s32[3]{0:T(128)}, u32[]{:S(2)}, u32[]{:S(2)}) collective-permute-start(s32[3]{0:T(128)} %get-tuple-element.57), channel_id=1, source_target_pairs={{0,2},{2,0},{4,6},{6,4},{8,10},{10,8},{12,14},{14,12},{16,18},{18,... | collective-permute-start | bytes 44 | tf_op jit(solution)/shard_map/ppermute | solution.py:31
  40.7 102.2 %collective-permute-start.1 = (s32[3]{0:T(128)}, s32[3]{0:T(128)}, u32[]{:S(2)}, u32[]{:S(2)}) collective-permute-start(s32[3]{0:T(128)} %get-tuple-element.56), channel_id=1, source_target_pairs={{0,4},{2,6},{4,0},{6,2},{8,12},{10,14},{12,8},{14,10},{16,20},{18,... | collective-permute-start | bytes 44 | tf_op jit(solution)/shard_map/ppermute | solution.py:31
  42.4 100.6 %collective-permute-start.2 = (s32[3]{0:T(128)}, s32[3]{0:T(128)}, u32[]{:S(2)}, u32[]{:S(2)}) collective-permute-start(s32[3]{0:T(128)} %get-tuple-element.55), channel_id=1, source_target_pairs={{0,6},{2,4},{4,2},{6,0},{8,14},{10,12},{12,10},{14,8},{16,22},{18,... | collective-permute-start | bytes 44 | tf_op jit(solution)/shard_map/ppermute | solution.py:31
  42.4 200.5 %collective-permute-start.3 = (s32[3]{0:T(128)}, s32[3]{0:T(128)}, u32[]{:S(2)}, u32[]{:S(2)}) collective-permute-start(s32[3]{0:T(128)} %get-tuple-element.54), channel_id=1, source_target_pairs={{0,8},{2,10},{4,12},{6,14},{8,0},{10,2},{12,4},{14,6},{16,24},{18,... | collective-permute-start | bytes 44 | tf_op jit(solution)/shard_map/ppermute | solution.py:31
  44.1 202.5 %collective-permute-start.4 = (s32[3]{0:T(128)}, s32[3]{0:T(128)}, u32[]{:S(2)}, u32[]{:S(2)}) collective-permute-start(s32[3]{0:T(128)} %get-tuple-element.53), channel_id=1, source_target_pairs={{0,10},{2,8},{4,14},{6,12},{8,2},{10,0},{12,6},{14,4},{16,26},{18,... | collective-permute-start | bytes 44 | tf_op jit(solution)/shard_map/ppermute | solution.py:31
  135.4 177.9 %copy-start.72 = (s32[3]{0:T(128)S(1)}, s32[3]{0:T(128)}, u32[]{:S(2)}) copy-start(s32[3]{0:T(128)} %get-tuple-element.45) | copy-start | bytes 40
  135.4 178.2 %copy-start.71 = (s32[3]{0:T(128)S(1)}, s32[3]{0:T(128)}, u32[]{:S(2)}) copy-start(s32[3]{0:T(128)} %get-tuple-element.44) | copy-start | bytes 40
  135.4 181.6 %copy-start.70 = (s32[3]{0:T(128)S(1)}, s32[3]{0:T(128)}, u32[]{:S(2)}) copy-start(s32[3]{0:T(128)} %get-tuple-element.43) | copy-start | bytes 40
  140.3 108.2 %collective-permute-start.5 = (s32[3]{0:T(128)S(1)}, s32[3]{0:T(128)S(1)}, u32[]{:S(2)}, u32[]{:S(2)}) collective-permute-start(s32[3]{0:T(128)S(1)} %copy-done.79), channel_id=1, source_target_pairs={{0,12},{2,14},{4,8},{6,10},{8,4},{10,6},{12,0},{14,2},{16,28},{18,... | collective-permute-start | bytes 44 | tf_op jit(solution)/shard_map/ppermute | solution.py:31
  143.0 107.8 %collective-permute-start.6 = (s32[3]{0:T(128)S(1)}, s32[3]{0:T(128)S(1)}, u32[]{:S(2)}, u32[]{:S(2)}) collective-permute-start(s32[3]{0:T(128)S(1)} %copy-done.78), channel_id=1, source_target_pairs={{0,14},{2,12},{4,10},{6,8},{8,6},{10,4},{12,2},{14,0},{16,30},{18,... | collective-permute-start | bytes 44 | tf_op jit(solution)/shard_map/ppermute | solution.py:31
  143.0 170.2 %collective-permute-start.7 = (s32[3]{0:T(128)S(1)}, s32[3]{0:T(128)S(1)}, u32[]{:S(2)}, u32[]{:S(2)}) collective-permute-start(s32[3]{0:T(128)S(1)} %copy-done.77), channel_id=1, source_target_pairs={{0,16},{2,18},{4,20},{6,22},{8,24},{10,26},{12,28},{14,30},{16,0},... | collective-permute-start | bytes 44 | tf_op jit(solution)/shard_map/ppermute | solution.py:31
  242.9 70.7 %collective-permute-start.8 = (s32[3]{0:T(128)S(1)}, s32[3]{0:T(128)S(1)}, u32[]{:S(2)}, u32[]{:S(2)}) collective-permute-start(s32[3]{0:T(128)S(1)} %copy-done.76), channel_id=1, source_target_pairs={{0,18},{2,16},{4,22},{6,20},{8,26},{10,24},{12,30},{14,28},{16,2},... | collective-permute-start | bytes 44 | tf_op jit(solution)/shard_map/ppermute | solution.py:31
  246.6 70.3 %collective-permute-start.9 = (s32[3]{0:T(128)S(1)}, s32[3]{0:T(128)S(1)}, u32[]{:S(2)}, u32[]{:S(2)}) collective-permute-start(s32[3]{0:T(128)S(1)} %copy-done.75), channel_id=1, source_target_pairs={{0,20},{2,22},{4,16},{6,18},{8,28},{10,30},{12,24},{14,26},{16,4},... | collective-permute-start | bytes 44 | tf_op jit(solution)/shard_map/ppermute | solution.py:31
  248.5 70.5 %collective-permute-start.10 = (s32[3]{0:T(128)S(1)}, s32[3]{0:T(128)S(1)}, u32[]{:S(2)}, u32[]{:S(2)}) collective-permute-start(s32[3]{0:T(128)S(1)} %copy-done.74), channel_id=1, source_target_pairs={{0,22},{2,20},{4,18},{6,16},{8,30},{10,28},{12,26},{14,24},{16,6},... | collective-permute-start | bytes 44 | tf_op jit(solution)/shard_map/ppermute | solution.py:31
  250.7 68.2 %collective-permute-start.11 = (s32[3]{0:T(128)S(1)}, s32[3]{0:T(128)S(1)}, u32[]{:S(2)}, u32[]{:S(2)}) collective-permute-start(s32[3]{0:T(128)S(1)} %copy-done.73), channel_id=1, source_target_pairs={{0,24},{2,26},{4,28},{6,30},{8,16},{10,18},{12,20},{14,22},{16,8},... | collective-permute-start | bytes 44 | tf_op jit(solution)/shard_map/ppermute | solution.py:31
  313.2 5.7 %collective-permute-start.12 = (s32[3]{0:T(128)S(1)}, s32[3]{0:T(128)S(1)}, u32[]{:S(2)}, u32[]{:S(2)}) collective-permute-start(s32[3]{0:T(128)S(1)} %copy-done.72), channel_id=1, source_target_pairs={{0,26},{2,24},{4,30},{6,28},{8,18},{10,16},{12,22},{14,20},{16,10}... | collective-permute-start | bytes 44 | tf_op jit(solution)/shard_map/ppermute | solution.py:31
  313.6 6.3 %collective-permute-start.13 = (s32[3]{0:T(128)S(1)}, s32[3]{0:T(128)S(1)}, u32[]{:S(2)}, u32[]{:S(2)}) collective-permute-start(s32[3]{0:T(128)S(1)} %copy-done.71), channel_id=1, source_target_pairs={{0,28},{2,30},{4,24},{6,26},{8,20},{10,22},{12,16},{14,18},{16,12}... | collective-permute-start | bytes 44 | tf_op jit(solution)/shard_map/ppermute | solution.py:31
  317.0 5.7 %collective-permute-start.14 = (s32[3]{0:T(128)S(1)}, s32[3]{0:T(128)S(1)}, u32[]{:S(2)}, u32[]{:S(2)}) collective-permute-start(s32[3]{0:T(128)S(1)} %copy-done.70), channel_id=1, source_target_pairs={{0,30},{2,28},{4,26},{6,24},{8,22},{10,20},{12,18},{14,16},{16,14}... | collective-permute-start | bytes 44 | tf_op jit(solution)/shard_map/ppermute | solution.py:31
  384.1 43.9 %all-gather.2.cloned.1.call-start = ((), (), s32[]{:S(2)}) async-start(), calls=%async_computation.5 | async-start | bytes 1572864 | tf_op jit(solution)/shard_map/all_gather | solution.py:185
  407.9 65.4 %reduce-scatter.5.cloned.1.call-start = ((), (), s32[]{:S(2)}) async-start(), calls=%async_computation.6 | async-start | bytes 1572864 | tf_op jit(solution)/shard_map/reduce_scatter | solution.py:189
  (88 other events, 1409.2 us)
Sparse Core Ops, SparseCore 0:
  384.2 18.9 reduce-scatter.2
  408.0 19.9 all-gather.1
  441.1 20.3 reduce-scatter.4
